TPU v7x, 32 devices: a whole 2x2x4 slice. The times are simulated.
32 devices in a mesh: dp: 16 (over z, y, x), head: 2 (over core).
Axes of the slice: x: 2, y: 2, z: 4, core: 2. Of those that a mesh axis runs over, the one named last changes fastest.
Arguments:
- patches: bfloat16 [16384, 768], P('dp'), may hold values from -6 to 6
- image_grids: int32 [96, 2], P('dp'), may hold values from 0 to 24, as said below
- out_grad: bfloat16 [16384, 768], P('dp'), may hold values from -6 to 6
- first_gain: float32 [768], replicated, may hold values from 0.5 to 1.5
- first_shift: float32 [768], replicated, may hold values from -1 to 1
- qkv_weight: bfloat16 [3, 768, 768], P(None, None, 'head'), may hold values from -0.21875 to 0.21875
- qkv_bias: float32 [3, 768], P(None, 'head'), may hold values from -1 to 1
- rope_freqs: float32 [2, 12, 32], P(None, 'head'), may hold values from -0.8 to 0.8
- proj_weight: bfloat16 [768, 768], P('head'), may hold values from -2.5 to 2.5
- proj_bias: float32 [768], replicated, may hold values from -1 to 1
- second_gain: float32 [768], replicated, may hold values from 0.5 to 1.5
- second_shift: float32 [768], replicated, may hold values from -1 to 1
- expand_weight: bfloat16 [768, 3072], P(None, 'head'), may hold values from -0.21875 to 0.21875
- expand_bias: float32 [3072], P('head'), may hold values from -1 to 1
- contract_weight: bfloat16 [3072, 768], P('head'), may hold values from -0.109375 to 0.109375
- contract_bias: float32 [768], replicated, may hold values from -1 to 1
Outputs:
- mixed_out: bfloat16 [16384, 768], P('dp')
- patches_grad: float32 [16384, 768], P('dp')
- qkv_weight_grad: float32 [3, 768, 768], P(None, 'dp', 'head')
- proj_weight_grad: float32 [768, 768], P('head', 'dp')
- expand_weight_grad: float32 [768, 3072], P('dp', 'head')
- contract_weight_grad: float32 [3072, 768], P('head', 'dp')
- first_gain_grad: float32 [768], replicated
- first_shift_grad: float32 [768], replicated
- qkv_bias_grad: float32 [3, 768], P(None, 'head')
- rope_freqs_grad: float32 [2, 12, 32], P(None, 'head')
- proj_bias_grad: float32 [768], replicated
- second_gain_grad: float32 [768], replicated
- second_shift_grad: float32 [768], replicated
- expand_bias_grad: float32 [3072], P('head')
- contract_bias_grad: float32 [768], replicated
Inputs may be any that keep to these rules, and one draw needn't show every extreme that they name: `image_grids`: every image is square with side 14, 20 or 24, height equal to width. In each block of 6 rows (one index of dp) the images come first and the empty slots (0, 0) after them; the images' patches total at most 1024, and every block has an empty slot.
All inputs are finite; a program needn't handle non-finite values.
Results may differ from a plain program's by a relative error of at most 0.012.
Values sent between devices are 32-bit elements; how exact they have to be, the bound alone decides.
A program may use at most 192 MiB of HBM per device.

v0:
```python
from functools import partial
import jax
import jax.numpy as jnp
from jax import lax
from jax.sharding import PartitionSpec as P

eps = 1e-06
masked_score = -1e30


def positions(image_grids, row_count):
    slot_count = image_grids.shape[0]
    image_len = image_grids[:, 0] * image_grids[:, 1]
    image_end = jnp.cumsum(image_len)
    image_start = image_end - image_len
    token_pos = jnp.arange(row_count, dtype=jnp.int32)
    segment = jnp.sum((token_pos[:, None] >= image_end[None, :]).astype(jnp.int32), axis=1)
    member = segment[:, None] == jnp.arange(slot_count, dtype=jnp.int32)[None, :]
    start_tok = jnp.sum(jnp.where(member, image_start[None, :], 0), axis=1)
    width_tok = jnp.sum(jnp.where(member, image_grids[None, :, 1], 0), axis=1)
    offset = token_pos - start_tok
    safe_width = jnp.maximum(width_tok, 1)
    real_row = segment < slot_count
    grid_row = jnp.where(real_row, offset // safe_width, 0).astype(jnp.float32)
    grid_col = jnp.where(real_row, offset % safe_width, 0).astype(jnp.float32)
    return (segment, grid_row, grid_col, real_row.astype(jnp.float32))


def layer_norm_parts(source, gain, shift):
    mean_val = jnp.mean(source, axis=-1, keepdims=True)
    centred = source - mean_val
    inv_dev = lax.rsqrt(jnp.mean(centred * centred, axis=-1, keepdims=True) + eps)
    unit = centred * inv_dev
    return (unit * gain + shift, unit, inv_dev)


def norm_back(upstream, unit, inv_dev, gain):
    scaled = upstream * gain
    return inv_dev * (
        scaled
        - jnp.mean(scaled, axis=-1, keepdims=True)
        - unit * jnp.mean(scaled * unit, axis=-1, keepdims=True)
    )


def rotate_pairs(source, cosine, sine_val):
    row_count = source.shape[0]
    head_count = cosine.shape[1]
    half_size = cosine.shape[2]
    shaped = source.reshape(row_count, head_count, 2, half_size)
    first_half = shaped[:, :, 0]
    second_half = shaped[:, :, 1]
    turned = jnp.stack(
        [
            first_half * cosine - second_half * sine_val,
            first_half * sine_val + second_half * cosine,
        ],
        axis=2,
    )
    return turned.reshape(row_count, head_count * 2 * half_size)


def rotate_back(grad_rot, turned, cosine, sine_val):
    row_count = grad_rot.shape[0]
    head_count = cosine.shape[1]
    half_size = cosine.shape[2]
    grad_shaped = grad_rot.reshape(row_count, head_count, 2, half_size)
    turn_shaped = turned.reshape(row_count, head_count, 2, half_size)
    grad_first = grad_shaped[:, :, 0]
    grad_second = grad_shaped[:, :, 1]
    input_grad = jnp.stack(
        [
            grad_first * cosine + grad_second * sine_val,
            grad_second * cosine - grad_first * sine_val,
        ],
        axis=2,
    )
    angle_grad = grad_second * turn_shaped[:, :, 0] - grad_first * turn_shaped[:, :, 1]
    return (input_grad.reshape(row_count, head_count * 2 * half_size), angle_grad)


def attend_forward(query_low, key_low, value_low, segment, head_count):
    row_count = query_low.shape[0]
    head_size = query_low.shape[1] // head_count
    block = min(512, row_count)
    count = row_count // block
    score_scale = head_size ** (-0.5)
    key_heads = key_low.reshape(row_count, head_count, head_size)
    value_heads = value_low.reshape(row_count, head_count, head_size)
    query_blocks = query_low.reshape(count, block, head_count, head_size)
    segment_blocks = segment.reshape(count, block)

    def one_block(block_item):
        query_block, segment_query = block_item
        scores = (
            jnp.einsum("qhd,khd->hqk", query_block, key_heads, preferred_element_type=jnp.float32)
            * score_scale
        )
        same_image = (segment_query[:, None] == segment[None, :])[None]
        scores = jnp.where(same_image, scores, masked_score)
        row_max = jnp.max(scores, axis=-1, keepdims=True)
        exp_scores = jnp.exp(scores - row_max)
        row_total = jnp.sum(exp_scores, axis=-1, keepdims=True)
        probabilities = (exp_scores / row_total).astype(jnp.bfloat16)
        block_out = jnp.einsum(
            "hqk,khd->qhd", probabilities, value_heads, preferred_element_type=jnp.float32
        )
        return (block_out, (row_max + jnp.log(row_total))[..., 0])

    block_outs, log_sum = lax.map(one_block, (query_blocks, segment_blocks))
    return (block_outs.reshape(row_count, head_count * head_size), log_sum)


def attend_backward(query_low, key_low, value_low, attended_grad, log_sum, segment, head_count):
    row_count = query_low.shape[0]
    head_size = query_low.shape[1] // head_count
    block = min(512, row_count)
    count = row_count // block
    score_scale = head_size ** (-0.5)
    key_heads = key_low.reshape(row_count, head_count, head_size)
    value_heads = value_low.reshape(row_count, head_count, head_size)
    query_blocks = query_low.reshape(count, block, head_count, head_size)
    grad_blocks = attended_grad.reshape(count, block, head_count, head_size)
    segment_blocks = segment.reshape(count, block)

    def one_block(carry, block_item):
        key_grad, value_grad = carry
        query_block, grad_block, log_block, segment_query = block_item
        scores = (
            jnp.einsum("qhd,khd->hqk", query_block, key_heads, preferred_element_type=jnp.float32)
            * score_scale
        )
        same_image = (segment_query[:, None] == segment[None, :])[None]
        scores = jnp.where(same_image, scores, masked_score)
        probabilities = jnp.exp(scores - log_block[..., None])
        value_grad = value_grad + jnp.einsum(
            "hqk,qhd->khd",
            probabilities.astype(jnp.bfloat16),
            grad_block,
            preferred_element_type=jnp.float32,
        )
        prob_grad = jnp.einsum(
            "qhd,khd->hqk", grad_block, value_heads, preferred_element_type=jnp.float32
        )
        inner = jnp.sum(probabilities * prob_grad, axis=-1, keepdims=True)
        score_grad = (probabilities * (prob_grad - inner)).astype(jnp.bfloat16)
        query_grad = (
            jnp.einsum("hqk,khd->qhd", score_grad, key_heads, preferred_element_type=jnp.float32)
            * score_scale
        )
        key_grad = (
            key_grad
            + jnp.einsum(
                "hqk,qhd->khd", score_grad, query_block, preferred_element_type=jnp.float32
            )
            * score_scale
        )
        return ((key_grad, value_grad), query_grad)

    empty = jnp.zeros((row_count, head_count, head_size), jnp.float32)
    (key_grad, value_grad), query_grads = lax.scan(
        one_block, (empty, empty), (query_blocks, grad_blocks, log_sum, segment_blocks)
    )
    width = head_count * head_size
    return (
        query_grads.reshape(row_count, width),
        key_grad.reshape(row_count, width),
        value_grad.reshape(row_count, width),
    )


def run_forward(source, params, cosine, sine_val, segment):
    (
        gain_one,
        shift_one,
        weight_qkv,
        bias_qkv,
        weight_proj,
        bias_proj,
        gain_two,
        shift_two,
        weight_expand,
        bias_expand,
        weight_contract,
        bias_contract,
    ) = params
    start_value = source.astype(jnp.float32)
    norm_one, unit_one, inv_one = layer_norm_parts(start_value, gain_one, shift_one)
    normed_first = norm_one.astype(jnp.bfloat16)
    projected = (
        jnp.einsum("td,kdh->kth", normed_first, weight_qkv, preferred_element_type=jnp.float32)
        + bias_qkv[:, None, :]
    )
    query_rot = rotate_pairs(projected[0], cosine, sine_val)
    key_rot = rotate_pairs(projected[1], cosine, sine_val)
    query_low = query_rot.astype(jnp.bfloat16)
    key_low = key_rot.astype(jnp.bfloat16)
    value_low = projected[2].astype(jnp.bfloat16)
    attended, log_sum = attend_forward(query_low, key_low, value_low, segment, cosine.shape[1])
    attended_low = attended.astype(jnp.bfloat16)
    branch = (
        lax.psum(jnp.dot(attended_low, weight_proj, preferred_element_type=jnp.float32), "head")
        + bias_proj
    )
    middle = start_value + branch
    norm_two, unit_two, inv_two = layer_norm_parts(middle, gain_two, shift_two)
    normed_second = norm_two.astype(jnp.bfloat16)
    hidden = jnp.dot(normed_second, weight_expand, preferred_element_type=jnp.float32) + bias_expand
    active_low = jax.nn.gelu(hidden, approximate=False).astype(jnp.bfloat16)
    branch_two = (
        lax.psum(jnp.dot(active_low, weight_contract, preferred_element_type=jnp.float32), "head")
        + bias_contract
    )
    outcome = middle + branch_two
    return (
        unit_one,
        inv_one,
        normed_first,
        query_rot,
        key_rot,
        query_low,
        key_low,
        value_low,
        log_sum,
        attended_low,
        unit_two,
        inv_two,
        normed_second,
        hidden,
        active_low,
        outcome,
    )


def body(
    patches,
    image_grids,
    out_grad,
    first_gain,
    first_shift,
    qkv_weight,
    qkv_bias,
    rope_freqs,
    proj_weight,
    proj_bias,
    second_gain,
    second_shift,
    expand_weight,
    expand_bias,
    contract_weight,
    contract_bias,
):
    row_count = patches.shape[0]
    head_count = rope_freqs.shape[1]
    segment, grid_row, grid_col, real_row = positions(image_grids, row_count)
    turn_angle = (
        grid_row[:, None, None] * rope_freqs[0][None]
        + grid_col[:, None, None] * rope_freqs[1][None]
    )
    cosine = jnp.cos(turn_angle)
    sine_val = jnp.sin(turn_angle)
    params = (
        first_gain,
        first_shift,
        qkv_weight,
        qkv_bias,
        proj_weight,
        proj_bias,
        second_gain,
        second_shift,
        expand_weight,
        expand_bias,
        contract_weight,
        contract_bias,
    )
    saved = run_forward(patches, params, cosine, sine_val, segment)
    mixed_out = saved[15].astype(jnp.bfloat16)
    fresh = lax.optimization_barrier((patches, params, mixed_out))
    saved = run_forward(fresh[0], fresh[1], cosine, sine_val, segment)
    (
        unit_one,
        inv_one,
        normed_first,
        query_rot,
        key_rot,
        query_low,
        key_low,
        value_low,
        log_sum,
        attended_low,
        unit_two,
        inv_two,
        normed_second,
        hidden,
        active_low,
        outcome,
    ) = saved
    cot_low = out_grad * real_row[:, None].astype(jnp.bfloat16)
    cot_value = cot_low.astype(jnp.float32)
    contract_bias_grad = jnp.sum(cot_value, axis=0)
    contract_grad = jnp.einsum("tf,td->fd", active_low, cot_low, preferred_element_type=jnp.float32)
    active_grad = jnp.einsum(
        "td,fd->tf", cot_low, contract_weight, preferred_element_type=jnp.float32
    )
    gelu_value, gelu_pull = jax.vjp(partial(jax.nn.gelu, approximate=False), hidden)
    hidden_grad = gelu_pull(active_grad)[0].astype(jnp.bfloat16)
    expand_bias_grad = jnp.sum(hidden_grad.astype(jnp.float32), axis=0)
    expand_grad = jnp.einsum(
        "td,tf->df", normed_second, hidden_grad, preferred_element_type=jnp.float32
    )
    second_grad = lax.psum(
        jnp.einsum("tf,df->td", hidden_grad, expand_weight, preferred_element_type=jnp.float32),
        "head",
    )
    second_gain_grad = jnp.sum(second_grad * unit_two, axis=0)
    second_shift_grad = jnp.sum(second_grad, axis=0)
    middle_grad = cot_value + norm_back(second_grad, unit_two, inv_two, second_gain)
    middle_low = middle_grad.astype(jnp.bfloat16)
    proj_bias_grad = jnp.sum(middle_low.astype(jnp.float32), axis=0)
    proj_grad = jnp.einsum(
        "th,td->hd", attended_low, middle_low, preferred_element_type=jnp.float32
    )
    attended_grad = jnp.einsum(
        "td,hd->th", middle_low, proj_weight, preferred_element_type=jnp.float32
    ).astype(jnp.bfloat16)
    query_rot_grad, key_rot_grad, value_grad = attend_backward(
        query_low, key_low, value_low, attended_grad, log_sum, segment, head_count
    )
    query_in_grad, query_angle = rotate_back(query_rot_grad, query_rot, cosine, sine_val)
    key_in_grad, key_angle = rotate_back(key_rot_grad, key_rot, cosine, sine_val)
    angle_grad = query_angle + key_angle
    rope_freqs_grad = jnp.stack(
        [
            jnp.einsum("t,thf->hf", grid_row, angle_grad, precision=lax.Precision.HIGHEST),
            jnp.einsum("t,thf->hf", grid_col, angle_grad, precision=lax.Precision.HIGHEST),
        ]
    )
    qkv_grad_low = jnp.stack([query_in_grad, key_in_grad, value_grad]).astype(jnp.bfloat16)
    qkv_bias_grad = jnp.sum(qkv_grad_low.astype(jnp.float32), axis=1)
    qkv_grad = jnp.einsum(
        "td,kth->kdh", normed_first, qkv_grad_low, preferred_element_type=jnp.float32
    )
    first_grad = lax.psum(
        jnp.einsum("kth,kdh->td", qkv_grad_low, qkv_weight, preferred_element_type=jnp.float32),
        "head",
    )
    first_gain_grad = jnp.sum(first_grad * unit_one, axis=0)
    first_shift_grad = jnp.sum(first_grad, axis=0)
    patches_grad = middle_grad + norm_back(first_grad, unit_one, inv_one, first_gain)
    qkv_sum, proj_sum, expand_sum, contract_sum = (
        lax.psum_scatter(qkv_grad, "dp", scatter_dimension=1, tiled=True),
        lax.psum_scatter(proj_grad, "dp", scatter_dimension=1, tiled=True),
        lax.psum_scatter(expand_grad, "dp", scatter_dimension=0, tiled=True),
        lax.psum_scatter(contract_grad, "dp", scatter_dimension=1, tiled=True),
    )
    (
        first_gain_sum,
        first_shift_sum,
        qkv_bias_sum,
        rope_freqs_sum,
        proj_bias_sum,
        second_gain_sum,
        second_shift_sum,
        expand_bias_sum,
        contract_bias_sum,
    ) = lax.psum(
        (
            first_gain_grad,
            first_shift_grad,
            qkv_bias_grad,
            rope_freqs_grad,
            proj_bias_grad,
            second_gain_grad,
            second_shift_grad,
            expand_bias_grad,
            contract_bias_grad,
        ),
        "dp",
    )
    return (
        mixed_out,
        patches_grad,
        qkv_sum,
        proj_sum,
        expand_sum,
        contract_sum,
        first_gain_sum,
        first_shift_sum,
        qkv_bias_sum,
        rope_freqs_sum,
        proj_bias_sum,
        second_gain_sum,
        second_shift_sum,
        expand_bias_sum,
        contract_bias_sum,
    )


def solution(mesh):
    in_specs = (
        P("dp", None),
        P("dp", None),
        P("dp", None),
        P(),
        P(),
        P(None, None, "head"),
        P(None, "head"),
        P(None, "head", None),
        P("head", None),
        P(),
        P(),
        P(),
        P(None, "head"),
        P("head"),
        P("head", None),
        P(),
    )
    out_specs = (
        P("dp", None),
        P("dp", None),
        P(None, "dp", "head"),
        P("head", "dp"),
        P("dp", "head"),
        P("head", "dp"),
        P(),
        P(),
        P(None, "head"),
        P(None, "head", None),
        P(),
        P(),
        P(),
        P("head"),
        P(),
    )
    return jax.shard_map(body, mesh=mesh, in_specs=in_specs, out_specs=out_specs, check_vma=False)
```

profile of v0, /device:TPU:0, one launch (start us, length us, event | category | flops | bytes accessed | tf_op | source)
XLA Modules:
  0.0 1078.4 jit_solution(5829515903000823336)
XLA Ops:
  13.6 3.8 add_bitcast_fusion.1
  19.4 4.5 subtract_convert_fusion.1
  29.6 64.2 %while.37 = (s32[]{:T(128)}, bf16[2,512,6,64]{1,3,2,0:T(8,128)(2,1)}, s32[2,512]{1,0:T(2,128)S(1)}, s32[1024]{0:T(1024)S(1)}, bf16[2,512,6,64]{1,3,2,0:T(8,128)(...) while((s32[]{:T(128)}, bf16[2,512,6,64]{1,3,2,0:T(8,128)(2,1)}, ...), condition=%wide.region_9.10_spmd, body=%wide.region_6.9_spmd.sunk | while | flops 830997504 | bytes 63609020 | solution.py:110
  30.0 7.4 fusion.243
  37.4 16.7 %fusion.244 = (f32[6,512]{1,0:T(8,128)S(1)}, f32[6,512,1024]{2,1,0:T(8,128)}) fusion(f32[6,512,1024]{2,1,0:T(8,128)} %fusion.243, pred[512,1024]{1,0:T(8,128)(4,1)S(1)} %broadcast_compare_fusion.8), kind=kOutput, calls=%fused_computation.303.clone.1 | output fusion | flops 18875392 | bytes 25702400 | tf_op jit(solution)/shard_map/while/body/eval_jaxpr/sub | solution.py:102
  54.1 6.7 fusion.245
  62.1 7.4 fusion.243
  69.5 16.7 %fusion.244 = (f32[6,512]{1,0:T(8,128)S(1)}, f32[6,512,1024]{2,1,0:T(8,128)}) fusion(f32[6,512,1024]{2,1,0:T(8,128)} %fusion.243, pred[512,1024]{1,0:T(8,128)(4,1)S(1)} %broadcast_compare_fusion.8), kind=kOutput, calls=%fused_computation.303.clone.1 | output fusion | flops 18875392 | bytes 25702400 | tf_op jit(solution)/shard_map/while/body/eval_jaxpr/sub | solution.py:102
  86.2 6.7 fusion.245
  98.7 26.1 %all-reduce.9.cloned.1.call-done = f32[1024,768]{1,0:T(8,128)} async-done(((f32[1024,768]{1,0:T(8,128)}), f32[1024,768]{1,0:T(8,128)}) %all-reduce.9.cloned.1.call-update) | async-done | bytes 3145744 | tf_op jit(solution)/shard_map/psum | solution.py:202
  129.5 21.6 %fusion.87 = f32[1024,768]{1,0:T(8,128)} fusion(bf16[1536,768]{1,0:T(8,128)(2,1)} %param.36, bf16[768,1536]{1,0:T(8,128)(2,1)S(1)} %copy-done, f32[1536]{0:T(1024)S(1)} %copy-done.70, f32[768]{0:T(1024)S(1)} %copy-done.77, f32[768]{0:T(1024)S(1)} %copy-done.56, f32[1024]{0:T(1024)S(1)} %add_rsqrt_fusion.2, f32[1024]{0:T(1024)S(1)} %broadcast_multiply_fusion.6, ...), kind=kOutput, calls=%fused_computation.148 | convolution fusion | flops 4941938688 | bytes 12606464 | tf_op jit(solution)/shard_map/dot_general | solution.py:211
  151.2 24.6 %all-reduce.11.cloned.1.call-done = f32[1024,768]{1,0:T(8,128)} async-done(((f32[1024,768]{1,0:T(8,128)}), f32[1024,768]{1,0:T(8,128)}) %all-reduce.11.cloned.1.call-update) | async-done | bytes 3145744 | tf_op jit(solution)/shard_map/psum | solution.py:211
  175.8 5.1 add_convert_fusion.2
  187.0 4.0 fusion.123
  198.6 25.5 %while.38 = (s32[]{:T(128)}, bf16[2,512,6,64]{1,3,2,0:T(8,128)(2,1)}, f32[2,6,512]{2,1,0:T(8,128)S(1)}, s32[2,512]{1,0:T(2,128)S(1)}, s32[1024]{0:T(1024)S(1)}, ...) while((s32[]{:T(128)}, ...), condition=%wide.region_19.20_spmd, body=%wide.region_16.19_spmd.sunk | while | flops 843576320 | bytes 52164808 | solution.py:110
  202.4 3.6 fusion.249
  206.1 4.4 fusion.250
  218.8 4.4 fusion.250
  230.1 24.4 %all-reduce.13.cloned.1.call-done = f32[1024,768]{1,0:T(8,128)} async-done(((f32[1024,768]{1,0:T(8,128)}), f32[1024,768]{1,0:T(8,128)}) %all-reduce.13.cloned.1.call-update) | async-done | bytes 3145744 | tf_op jit(solution)/shard_map/psum | solution.py:202
  257.9 15.1 %fusion.51 = (f32[1024,1536]{1,0:T(8,128)S(1)}, f32[1024,1536]{1,0:T(8,128)S(1)}) fusion(f32[1536]{0:T(1024)S(1)} %copy-done.70, bf16[768,1536]{1,0:T(8,128)(2,1)S(1)} %copy-done, f32[1024,768]{1,0:T(8,128)S(1)} %get-tuple-element.484, f32[768]{0:T(1024)S(1)} %copy-done.77, f32[768]{0:T(1024)S(1)} %copy-done.56, f32[1024]{0:T(1024)S(1)} %add_rsqrt_fusion, ...), kind=kOutput, calls=%fused_computation.70 | convolution fusion | flops 2518941696 | bytes 18108416 | tf_op jit(solution)/shard_map/dot_general | solution.py:208
  273.1 5.6 convert_reduce_fusion
  280.5 4.3 fusion.186
  284.9 24.6 %all-reduce.15.cloned.1.call-done = f32[1024,768]{1,0:T(8,128)} async-done(((f32[1024,768]{1,0:T(8,128)}), f32[1024,768]{1,0:T(8,128)}) %all-reduce.15.cloned.1.call-update) | async-done | bytes 3145744 | tf_op jit(solution)/shard_map/psum | solution.py:311
  309.4 4.4 multiply_reduce_fusion.1
  314.1 3.9 convert_reduce_fusion.5
  329.2 87.9 %while.39 = (s32[]{:T(128)}, f32[1024,6,64]{0,2,1:T(8,128)}, f32[1024,6,64]{0,2,1:T(8,128)}, f32[2,512,6,64]{1,0,3,2:T(2,128)}, bf16[2,512,6,64]{1,3,2,0:T(8,128...) while((s32[]{:T(128)}, f32[1024,6,64]{0,2,1:T(8,128)}, ...), condition=%wide.region_28.29_spmd.clone, body=%wide.region_26.28_spmd.clone.sunk | while | flops 2063135744 | bytes 132749616 | solution.py:161
  333.0 4.6 bitcast_add_fusion.5
  337.6 7.1 multiply_reduce_fusion.8
  344.7 6.9 multiply_convert_fusion.4
  357.9 15.0 %dynamic_update_slice.25 = f32[2,512,6,64]{1,0,3,2:T(2,128)} dynamic-update-slice(f32[2,512,6,64]{1,0,3,2:T(2,128)} %get-tuple-element.762, f32[1,512,6,64]{1,0,3,2:T(1,128)} %copy.267, s32[]{:T(128)S(6)} %copy.295, s32[]{:T(128)} %constant.51.clone.1..sunk, s32[]{:T(128)} %constant.51.clone.1..sunk, s32[]{:T(128)} %constant.51.clone.1..sunk) | dynamic-update-slice | bytes 1572868 | tf_op jit(solution)/shard_map/while/body/jit(dynamic_update_index_in_dim)/dynamic_update_slice | solution.py:110
  376.1 5.8 bitcast_add_fusion.5
  381.9 7.1 multiply_reduce_fusion.8
  389.0 6.9 multiply_convert_fusion.4
  402.2 15.0 %dynamic_update_slice.25 = f32[2,512,6,64]{1,0,3,2:T(2,128)} dynamic-update-slice(f32[2,512,6,64]{1,0,3,2:T(2,128)} %get-tuple-element.762, f32[1,512,6,64]{1,0,3,2:T(1,128)} %copy.267, s32[]{:T(128)S(6)} %copy.295, s32[]{:T(128)} %constant.51.clone.1..sunk, s32[]{:T(128)} %constant.51.clone.1..sunk, s32[]{:T(128)} %constant.51.clone.1..sunk) | dynamic-update-slice | bytes 1572868 | tf_op jit(solution)/shard_map/while/body/jit(dynamic_update_index_in_dim)/dynamic_update_slice | solution.py:110
  420.7 5.4 fusion.119
  438.0 5.9 convolution_bitcast_fusion.1
  444.6 6.1 convolution_bitcast_fusion
  450.7 6.5 copy.223
  458.3 3.9 fusion.142
  462.6 11.4 %fusion.84 = f32[1536,768]{0,1:T(8,128)} fusion(f32[1024,1536]{1,0:T(8,128)} %copy-done.80, f32[1024,1536]{1,0:T(8,128)} %copy-done.81, f32[1536]{0:T(1024)S(1)} %copy-done.71, bf16[1024,768]{1,0:T(8,128)(2,1)} %param.24, bf16[1024]{0:T(1024)(128)(2,1)S(1)} %copy-done.64), kind=kOutput, calls=%fused_computation.133 | convolution fusion | flops 2422996992 | bytes 18882560 | tf_op jit(solution)/shard_map/tf,td->fd/dot_general | solution.py:301
  474.7 7.9 fusion.177
  484.6 5.8 fusion.111
  497.5 79.5 %all-reduce.1 = (f32[768]{0:T(1024)}, f32[768]{0:T(1024)}, f32[3,384]{1,0:T(4,128)}, f32[2,6,32]{2,1,0:T(8,128)S(1)}, f32[768]{0:T(1024)}, /*index=5*/f32[768]{0...) all-reduce(f32[768]{0:T(1024)S(1)} %get-tuple-element.410, ...), channel_id=1, replica_groups=mesh['dp'=16,'head'=2] {'dp'}, use_global_device_ids=true, to_apply=%region_37.38 | all-reduce | flops 7680 | bytes 61440 | tf_op jit(solution)/shard_map/psum | solution.py:366
  577.6 5.0 fusion.77
  582.6 72.6 %all-reduce.19.cloned.1.call-done = f32[3,768,384]{2,0,1:T(4,128)} async-done(((f32[3,768,384]{2,0,1:T(4,128)}), f32[3,768,384]{2,0,1:T(4,128)}) %all-reduce.19.cloned.1.call-update) | async-done | bytes 3538960
  656.9 127.7 %reduce-scatter.4.cloned.1.call-done = f32[384,48]{0,1:T(8,128)} async-done(((f32[384,768]{0,1:T(8,128)}), f32[384,48]{0,1:T(8,128)}) %reduce-scatter.4.cloned.1.call-update) | async-done | bytes 73744 | tf_op jit(solution)/shard_map/reduce_scatter | solution.py:352
  784.6 143.5 %reduce-scatter.8.cloned.1.call-done = f32[1536,48]{0,1:T(8,128)} async-done(((f32[1536,768]{0,1:T(8,128)}), f32[1536,48]{0,1:T(8,128)}) %reduce-scatter.8.cloned.1.call-update) | async-done | bytes 294928 | tf_op jit(solution)/shard_map/reduce_scatter | solution.py:354
  928.1 143.6 %reduce-scatter.6.cloned.1.call-done = f32[48,1536]{1,0:T(8,128)} async-done(((f32[768,1536]{1,0:T(8,128)}), f32[48,1536]{1,0:T(8,128)}) %reduce-scatter.6.cloned.1.call-update) | async-done | bytes 294928 | tf_op jit(solution)/shard_map/reduce_scatter | solution.py:353
  (315 shorter events, 122.5 us)
Async XLA Ops:
  7.2 122.3 %copy-start = (bf16[768,1536]{1,0:T(8,128)(2,1)S(1)}, bf16[768,1536]{1,0:T(8,128)(2,1)}, u32[]{:S(2)}) copy-start(bf16[768,1536]{1,0:T(8,128)(2,1)} %param.34) | copy-start | bytes 7077892
  7.2 6.4 copy-start.58
  7.2 6.4 copy-start.72
  7.2 6.4 copy-start.74
  7.2 117.6 %all-reduce.9.cloned.1.call-start = ((), (), s32[]{:S(2)}) async-start(), calls=%async_computation.3 | async-start | bytes 6291456 | tf_op jit(solution)/shard_map/psum | solution.py:202
  9.7 3.9 copy-start.1
  19.1 4.8 copy-start.39
  19.2 4.8 copy-start.42
  19.4 4.5 copy-start.33
  19.4 4.5 copy-start.36
  37.4 16.7 %copy-start.25 = (bf16[2,512,6,64]{1,3,2,0:T(8,128)(2,1)S(1)}, bf16[2,512,6,64]{1,3,2,0:T(8,128)(2,1)}, u32[]{:S(2)}) copy-start(bf16[2,512,6,64]{1,3,2,0:T(8,128)(2,1)} %get-tuple-element.704) | copy-start | bytes 2359300 | tf_op jit(solution)/shard_map/while
  37.4 16.7 %copy-start.32 = (bf16[1024,6,64]{0,2,1:T(8,128)(2,1)S(1)}, bf16[1024,6,64]{0,2,1:T(8,128)(2,1)}, u32[]{:S(2)}) copy-start(bf16[1024,6,64]{0,2,1:T(8,128)(2,1)} %get-tuple-element.717) | copy-start | bytes 2359300 | tf_op jit(solution)/shard_map/while
  69.5 16.7 %copy-start.25 = (bf16[2,512,6,64]{1,3,2,0:T(8,128)(2,1)S(1)}, bf16[2,512,6,64]{1,3,2,0:T(8,128)(2,1)}, u32[]{:S(2)}) copy-start(bf16[2,512,6,64]{1,3,2,0:T(8,128)(2,1)} %get-tuple-element.704) | copy-start | bytes 2359300 | tf_op jit(solution)/shard_map/while
  69.5 16.7 %copy-start.32 = (bf16[1024,6,64]{0,2,1:T(8,128)(2,1)S(1)}, bf16[1024,6,64]{0,2,1:T(8,128)(2,1)}, u32[]{:S(2)}) copy-start(bf16[1024,6,64]{0,2,1:T(8,128)(2,1)} %get-tuple-element.717) | copy-start | bytes 2359300 | tf_op jit(solution)/shard_map/while
  96.0 28.9 %copy-start.49 = (f32[768]{0:T(1024)S(1)}, f32[768]{0:T(1024)}, u32[]{:S(2)}) copy-start(f32[768]{0:T(1024)} %param.31) | copy-start | bytes 9220
  98.7 77.1 %all-reduce.11.cloned.1.call-start = ((), (), s32[]{:S(2)}) async-start(), calls=%async_computation.4 | async-start | bytes 6291456 | tf_op jit(solution)/shard_map/psum | solution.py:211
  151.1 24.7 %copy-start.67 = (f32[768]{0:T(1024)S(1)}, f32[768]{0:T(1024)}, u32[]{:S(2)}) copy-start(f32[768]{0:T(1024)} %param.37) | copy-start | bytes 9220
  151.1 103.4 %all-reduce.13.cloned.1.call-start = ((), (), s32[]{:S(2)}) async-start(), calls=%async_computation.5 | async-start | bytes 6291456 | tf_op jit(solution)/shard_map/psum | solution.py:202
  175.8 5.1 copy-start.3
  181.2 4.0 copy-start.45
  186.7 4.4 copy-start.14
  186.7 4.4 copy-start.15
  229.9 79.5 %all-reduce.15.cloned.1.call-start = ((), (), s32[]{:S(2)}) async-start(), calls=%async_computation.6 | async-start | bytes 6291456 | tf_op jit(solution)/shard_map/psum | solution.py:311
  257.4 15.7 %copy-start.9 = (f32[1024,768]{1,0:T(8,128)}, f32[1024,768]{1,0:T(8,128)S(1)}, u32[]{:S(2)}) copy-start(f32[1024,768]{1,0:T(8,128)S(1)} %get-tuple-element.484) | copy-start | bytes 9437188
  257.4 56.5 %copy-start.47 = (f32[1024]{0:T(1024)}, f32[1024]{0:T(1024)S(1)}, u32[]{:S(2)}) copy-start(f32[1024]{0:T(1024)S(1)} %broadcast_multiply_fusion.4) | copy-start | bytes 12292
  257.9 56.0 %copy-start.52 = (f32[1024]{0:T(1024)}, f32[1024]{0:T(1024)S(1)}, u32[]{:S(2)}) copy-start(f32[1024]{0:T(1024)S(1)} %add_rsqrt_fusion) | copy-start | bytes 12292
  257.9 15.2 %copy-start.31 = (bf16[1024,768]{1,0:T(8,128)(2,1)S(1)}, bf16[1024,768]{1,0:T(8,128)(2,1)}, u32[]{:S(2)}) copy-start(bf16[1024,768]{1,0:T(8,128)(2,1)} %param.24) | copy-start | bytes 4718596
  257.9 15.2 %copy-start.63 = (bf16[1024]{0:T(1024)(128)(2,1)S(1)}, bf16[1024]{0:T(1024)(128)(2,1)}, u32[]{:S(2)}) copy-start(bf16[1024]{0:T(1024)(128)(2,1)} %get-tuple-element.481) | copy-start | bytes 6148
  257.9 15.2 %copy-start.68 = (bf16[1536,768]{1,0:T(8,128)(2,1)S(1)}, bf16[1536,768]{1,0:T(8,128)(2,1)}, u32[]{:S(2)}) copy-start(bf16[1536,768]{1,0:T(8,128)(2,1)} %param.36) | copy-start | bytes 7077892
  273.1 5.7 copy-start.80
  273.1 5.7 copy-start.81
  284.8 209.4 %all-reduce.17.cloned.1.call-start = ((), (), s32[]{:S(2)}) async-start(), calls=%async_computation.7 | async-start | bytes 6291456 | tf_op jit(solution)/shard_map/psum | solution.py:343
  309.4 4.5 copy-start.10
  309.4 4.7 copy-start.16
  314.1 5.5 copy-start.22
  333.0 4.6 copy-start.12
  376.1 5.8 copy-start.12
  420.7 5.4 copy-start.6
  433.1 4.9 copy-start.27
  443.9 211.3 %all-reduce.19.cloned.1.call-start = ((), (), s32[]{:S(2)}) async-start(), calls=%async_computation.11 | async-start | bytes 9437184
  457.2 5.3 copy-start.64
  457.2 5.3 copy-start.71
  457.2 327.3 %reduce-scatter.4.cloned.1.call-start = ((), (), s32[]{:S(2)}) async-start(), calls=%async_computation.8 | async-start | bytes 1253376 | tf_op jit(solution)/shard_map/reduce_scatter | solution.py:352
  462.3 465.8 %reduce-scatter.8.cloned.1.call-start = ((), (), s32[]{:S(2)}) async-start(), calls=%async_computation.10 | async-start | bytes 5013504 | tf_op jit(solution)/shard_map/reduce_scatter | solution.py:354
  474.0 597.6 %reduce-scatter.6.cloned.1.call-start = ((), (), s32[]{:S(2)}) async-start(), calls=%async_computation.9 | async-start | bytes 5013504 | tf_op jit(solution)/shard_map/reduce_scatter | solution.py:353
  484.5 9.2 copy-start.28
  484.5 9.2 copy-start.29
  484.6 9.2 copy-start.30
  (55 other events, 107.4 us)
Sparse Core Ops, SparseCore 0:
  98.8 26.0 all-reduce.8
  151.2 24.5 all-reduce.10
  230.0 24.4 all-reduce.12
  284.9 24.4 all-reduce.14
  444.0 24.4 all-reduce.16
  474.1 181.0 all-reduce.18
  660.5 124.0 reduce-scatter.3
  790.3 137.6 reduce-scatter.7
  933.8 137.7 reduce-scatter.5
where the time goes:
time: 1090 us; the launch traced here: 1080 us
  waiting for transfers between devices  587 us (54%)
  matrix products  180 us (17%)
  other arithmetic  121 us (11%)
  local copies, waits for them, and re-layouts  93.3 us (9%)
  blocking collectives  79.5 us (7%)
  between operations  15.7 us (1%)
    reduce_scatter x1, waiting for transfers between devices, body(): lax.psum_scatter(expand_grad, 'dp', scatter_dimension=0, tiled=True)  144 us
    reduce_scatter x1, waiting for transfers between devices, body(): lax.psum_scatter(contract_grad, 'dp', scatter_dimension=1, tiled=True)  143 us
    reduce_scatter x1, waiting for transfers between devices, body(): lax.psum_scatter(proj_grad, 'dp', scatter_dimension=1, tiled=True)  128 us
    psum x1, blocking collectives, body(): lax.psum((first_gain_grad, first_shift_grad, qkv_bias_grad, rope_freqs_gr...  79.5 us
    unnamed x10, waiting for transfers between devices  72.7 us
    psum x2, waiting for transfers between devices, run_forward(): lax.psum(jnp.dot(attended_low, weight_proj, preferred_element_type=jnp.fl...  50.6 us
    sub x2, other arithmetic, one_block(): exp_scores = jnp.exp(scores - row_max)  33.5 us
    dynamic_update_slice x4, local copies, waits for them, and re-layouts, attend_forward(): block_outs, log_sum = lax.map(one_block, (query_blocks, segment_blocks))  33.3 us
  transfers between devices with their start and end apart: 9, of which 8 were waited for; matrix products, arithmetic and copies ran while one was open for 5% of the time, Pallas kernels for 0%

commit v1 on v0

--- a/solution.py
+++ b/solution.py
@@ -199,7 +199,12 @@
     attended, log_sum = attend_forward(query_low, key_low, value_low, segment, cosine.shape[1])
     attended_low = attended.astype(jnp.bfloat16)
     branch = (
-        lax.psum(jnp.dot(attended_low, weight_proj, preferred_element_type=jnp.float32), "head")
+        jnp.sum(
+            lax.all_gather(
+                jnp.dot(attended_low, weight_proj, preferred_element_type=jnp.float32), "head"
+            ),
+            axis=0,
+        )
         + bias_proj
     )
     middle = start_value + branch

time: 1090 us -> 1080 us (level)
  waiting for transfers between devices: 587 us -> 574 us
    psum x2 -> x0, waiting for transfers between devices: 50.6 us -> none  [run_forward(): lax.psum(jnp.dot(attended_low, weight_proj, preferred_element_type=jnp.fl...]
    all_gather x0 -> x2, waiting for transfers between devices: none -> 37.3 us  [run_forward(): lax.all_gather(jnp.dot(attended_low, weight_proj, preferred_element_type=...]
where the time goes in v1:
time: 1080 us
  waiting for transfers between devices  574 us (53%)
  matrix products  180 us (17%)
  other arithmetic  131 us (12%)
  local copies, waits for them, and re-layouts  93.8 us (9%)
  blocking collectives  79.4 us (7%)
  between operations  15.7 us (1%)
    reduce_scatter x1, waiting for transfers between devices, body(): lax.psum_scatter(expand_grad, 'dp', scatter_dimension=0, tiled=True)  144 us
    reduce_scatter x1, waiting for transfers between devices, body(): lax.psum_scatter(contract_grad, 'dp', scatter_dimension=1, tiled=True)  143 us
    reduce_scatter x1, waiting for transfers between devices, body(): lax.psum_scatter(proj_grad, 'dp', scatter_dimension=1, tiled=True)  128 us
    psum x1, blocking collectives, body(): lax.psum((first_gain_grad, first_shift_grad, qkv_bias_grad, rope_freqs_gr...  79.4 us
    unnamed x10, waiting for transfers between devices  72.8 us
    all_gather x2, waiting for transfers between devices, run_forward(): lax.all_gather(jnp.dot(attended_low, weight_proj, preferred_element_type=...  37.3 us
    dynamic_update_slice x4, local copies, waits for them, and re-layouts, attend_forward(): block_outs, log_sum = lax.map(one_block, (query_blocks, segment_blocks))  33.4 us
    sub x2, other arithmetic, one_block(): exp_scores = jnp.exp(scores - row_max)  33.3 us
  transfers between devices with their start and end apart: 9, of which 8 were waited for; matrix products, arithmetic and copies ran while one was open for 5% of the time, Pallas kernels for 0%

profile of v1, /device:TPU:0, one launch (start us, length us, event | category | flops | bytes accessed | tf_op | source)
XLA Modules:
  0.0 1075.8 jit_solution(6451969139869441404)
XLA Ops:
  13.6 3.8 add_bitcast_fusion.1
  19.4 4.8 subtract_convert_fusion.1
  29.9 64.1 %while.37 = (s32[]{:T(128)}, bf16[2,512,6,64]{1,3,2,0:T(8,128)(2,1)}, s32[2,512]{1,0:T(2,128)S(1)}, s32[1024]{0:T(1024)S(1)}, bf16[2,512,6,64]{1,3,2,0:T(8,128)(...) while((s32[]{:T(128)}, bf16[2,512,6,64]{1,3,2,0:T(8,128)(2,1)}, ...), condition=%wide.region_9.10_spmd, body=%wide.region_6.9_spmd.sunk | while | flops 830997504 | bytes 63609020 | solution.py:110
  30.2 7.4 fusion.243
  37.6 16.7 %fusion.244 = (f32[6,512]{1,0:T(8,128)S(1)}, f32[6,512,1024]{2,1,0:T(8,128)}) fusion(f32[6,512,1024]{2,1,0:T(8,128)} %fusion.243, pred[512,1024]{1,0:T(8,128)(4,1)S(1)} %broadcast_compare_fusion.8), kind=kOutput, calls=%fused_computation.303.clone.1 | output fusion | flops 18875392 | bytes 25702400 | tf_op jit(solution)/shard_map/while/body/eval_jaxpr/sub | solution.py:102
  54.3 6.7 fusion.245
  62.3 7.4 fusion.243
  69.7 16.7 %fusion.244 = (f32[6,512]{1,0:T(8,128)S(1)}, f32[6,512,1024]{2,1,0:T(8,128)}) fusion(f32[6,512,1024]{2,1,0:T(8,128)} %fusion.243, pred[512,1024]{1,0:T(8,128)(4,1)S(1)} %broadcast_compare_fusion.8), kind=kOutput, calls=%fused_computation.303.clone.1 | output fusion | flops 18875392 | bytes 25702400 | tf_op jit(solution)/shard_map/while/body/eval_jaxpr/sub | solution.py:102
  86.3 6.7 fusion.245
  99.0 19.4 %all-gather.5.cloned.1.call-done = f32[2048,768]{1,0:T(8,128)} async-done(((f32[1024,768]{1,0:T(8,128)}), f32[2048,768]{1,0:T(8,128)}) %all-gather.5.cloned.1.call-update) | async-done | bytes 6291472 | tf_op jit(solution)/shard_map/all_gather | solution.py:203
  118.4 5.2 reduce_sum.257
  128.3 21.5 %fusion.87 = f32[1024,768]{1,0:T(8,128)} fusion(bf16[1536,768]{1,0:T(8,128)(2,1)} %param.36, bf16[768,1536]{1,0:T(8,128)(2,1)S(1)} %copy-done, f32[1536]{0:T(1024)S(1)} %copy-done.71, f32[768]{0:T(1024)S(1)} %copy-done.79, f32[768]{0:T(1024)S(1)} %copy-done.56, f32[1024]{0:T(1024)S(1)} %add_rsqrt_fusion.2, f32[1024]{0:T(1024)S(1)} %broadcast_multiply_fusion.6, ...), kind=kOutput, calls=%fused_computation.148 | convolution fusion | flops 4941938688 | bytes 12606464 | tf_op jit(solution)/shard_map/dot_general | solution.py:216
  150.3 24.2 %all-reduce.7.cloned.1.call-done = f32[1024,768]{1,0:T(8,128)} async-done(((f32[1024,768]{1,0:T(8,128)}), f32[1024,768]{1,0:T(8,128)}) %all-reduce.7.cloned.1.call-update) | async-done | bytes 3145744 | tf_op jit(solution)/shard_map/psum | solution.py:216
  174.5 5.1 add_convert_fusion.2
  196.9 25.5 %while.38 = (s32[]{:T(128)}, bf16[2,512,6,64]{1,3,2,0:T(8,128)(2,1)}, f32[2,6,512]{2,1,0:T(8,128)S(1)}, s32[2,512]{1,0:T(2,128)S(1)}, s32[1024]{0:T(1024)S(1)}, ...) while((s32[]{:T(128)}, ...), condition=%wide.region_19.20_spmd, body=%wide.region_16.19_spmd.sunk | while | flops 843576320 | bytes 52164808 | solution.py:110
  204.3 4.4 fusion.250
  217.1 4.4 fusion.250
  228.4 17.9 %all-gather.7.cloned.1.call-done = f32[2048,768]{1,0:T(8,128)} async-done(((f32[1024,768]{1,0:T(8,128)}), f32[2048,768]{1,0:T(8,128)}) %all-gather.7.cloned.1.call-update) | async-done | bytes 6291472 | tf_op jit(solution)/shard_map/all_gather | solution.py:203
  246.2 5.2 reduce_sum.262
  255.1 15.1 %fusion.51 = (f32[1024,1536]{1,0:T(8,128)S(1)}, f32[1024,1536]{1,0:T(8,128)S(1)}) fusion(f32[1536]{0:T(1024)S(1)} %copy-done.72, bf16[768,1536]{1,0:T(8,128)(2,1)S(1)} %copy-done, f32[1024,768]{1,0:T(8,128)S(1)} %get-tuple-element.484, f32[768]{0:T(1024)S(1)} %copy-done.80, f32[768]{0:T(1024)S(1)} %copy-done.57, f32[1024]{0:T(1024)S(1)} %add_rsqrt_fusion, ...), kind=kOutput, calls=%fused_computation.70 | convolution fusion | flops 2518941696 | bytes 18108416 | tf_op jit(solution)/shard_map/dot_general | solution.py:213
  270.3 5.6 convert_reduce_fusion
  277.6 4.3 fusion.186
  282.0 24.6 %all-reduce.9.cloned.1.call-done = f32[1024,768]{1,0:T(8,128)} async-done(((f32[1024,768]{1,0:T(8,128)}), f32[1024,768]{1,0:T(8,128)}) %all-reduce.9.cloned.1.call-update) | async-done | bytes 3145744 | tf_op jit(solution)/shard_map/psum | solution.py:316
  306.6 4.5 multiply_reduce_fusion.1
  311.3 3.9 convert_reduce_fusion.5
  326.5 88.0 %while.39 = (s32[]{:T(128)}, f32[1024,6,64]{0,2,1:T(8,128)}, f32[1024,6,64]{0,2,1:T(8,128)}, f32[2,512,6,64]{1,0,3,2:T(2,128)}, bf16[2,512,6,64]{1,3,2,0:T(8,128...) while((s32[]{:T(128)}, f32[1024,6,64]{0,2,1:T(8,128)}, ...), condition=%wide.region_28.29_spmd.clone, body=%wide.region_26.28_spmd.clone.sunk | while | flops 2063135744 | bytes 132749616 | solution.py:161
  330.2 4.6 bitcast_add_fusion.5
  334.8 7.2 multiply_reduce_fusion.8
  342.0 6.9 multiply_convert_fusion.4
  355.1 15.0 %dynamic_update_slice.25 = f32[2,512,6,64]{1,0,3,2:T(2,128)} dynamic-update-slice(f32[2,512,6,64]{1,0,3,2:T(2,128)} %get-tuple-element.762, f32[1,512,6,64]{1,0,3,2:T(1,128)} %copy.269, s32[]{:T(128)S(6)} %copy.295, s32[]{:T(128)} %constant.51.clone.1..sunk, s32[]{:T(128)} %constant.51.clone.1..sunk, s32[]{:T(128)} %constant.51.clone.1..sunk) | dynamic-update-slice | bytes 1572868 | tf_op jit(solution)/shard_map/while/body/jit(dynamic_update_index_in_dim)/dynamic_update_slice | solution.py:110
  373.4 5.8 bitcast_add_fusion.5
  379.2 7.2 multiply_reduce_fusion.8
  386.4 6.9 multiply_convert_fusion.4
  399.5 15.0 %dynamic_update_slice.25 = f32[2,512,6,64]{1,0,3,2:T(2,128)} dynamic-update-slice(f32[2,512,6,64]{1,0,3,2:T(2,128)} %get-tuple-element.762, f32[1,512,6,64]{1,0,3,2:T(1,128)} %copy.269, s32[]{:T(128)S(6)} %copy.295, s32[]{:T(128)} %constant.51.clone.1..sunk, s32[]{:T(128)} %constant.51.clone.1..sunk, s32[]{:T(128)} %constant.51.clone.1..sunk) | dynamic-update-slice | bytes 1572868 | tf_op jit(solution)/shard_map/while/body/jit(dynamic_update_index_in_dim)/dynamic_update_slice | solution.py:110
  418.1 5.4 fusion.119
  435.4 5.9 convolution_bitcast_fusion.1
  442.0 6.1 convolution_bitcast_fusion
  448.1 6.5 copy.223
  455.8 3.9 fusion.142
  460.0 11.4 %fusion.84 = f32[1536,768]{0,1:T(8,128)} fusion(f32[1024,1536]{1,0:T(8,128)} %copy-done.83, f32[1024,1536]{1,0:T(8,128)} %copy-done.84, f32[1536]{0:T(1024)S(1)} %copy-done.73, bf16[1024,768]{1,0:T(8,128)(2,1)} %param.24, bf16[1024]{0:T(1024)(128)(2,1)S(1)} %copy-done.65), kind=kOutput, calls=%fused_computation.133 | convolution fusion | flops 2422996992 | bytes 18882560 | tf_op jit(solution)/shard_map/tf,td->fd/dot_general | solution.py:306
  472.1 8.0 fusion.177
  482.0 5.8 fusion.111
  494.9 79.4 %all-reduce.1 = (f32[768]{0:T(1024)}, f32[768]{0:T(1024)}, f32[3,384]{1,0:T(4,128)}, f32[2,6,32]{2,1,0:T(8,128)S(1)}, f32[768]{0:T(1024)}, /*index=5*/f32[768]{0...) all-reduce(f32[768]{0:T(1024)S(1)} %get-tuple-element.410, ...), channel_id=1, replica_groups=mesh['dp'=16,'head'=2] {'dp'}, use_global_device_ids=true, to_apply=%region_37.38 | all-reduce | flops 7680 | bytes 61440 | tf_op jit(solution)/shard_map/psum | solution.py:371
  574.9 5.0 fusion.77
  579.9 72.7 %all-reduce.13.cloned.1.call-done = f32[3,768,384]{2,0,1:T(4,128)} async-done(((f32[3,768,384]{2,0,1:T(4,128)}), f32[3,768,384]{2,0,1:T(4,128)}) %all-reduce.13.cloned.1.call-update) | async-done | bytes 3538960
  654.3 127.7 %reduce-scatter.4.cloned.1.call-done = f32[384,48]{0,1:T(8,128)} async-done(((f32[384,768]{0,1:T(8,128)}), f32[384,48]{0,1:T(8,128)}) %reduce-scatter.4.cloned.1.call-update) | async-done | bytes 73744 | tf_op jit(solution)/shard_map/reduce_scatter | solution.py:357
  782.0 143.5 %reduce-scatter.8.cloned.1.call-done = f32[1536,48]{0,1:T(8,128)} async-done(((f32[1536,768]{0,1:T(8,128)}), f32[1536,48]{0,1:T(8,128)}) %reduce-scatter.8.cloned.1.call-update) | async-done | bytes 294928 | tf_op jit(solution)/shard_map/reduce_scatter | solution.py:359
  925.5 143.6 %reduce-scatter.6.cloned.1.call-done = f32[48,1536]{1,0:T(8,128)} async-done(((f32[768,1536]{1,0:T(8,128)}), f32[48,1536]{1,0:T(8,128)}) %reduce-scatter.6.cloned.1.call-update) | async-done | bytes 294928 | tf_op jit(solution)/shard_map/reduce_scatter | solution.py:358
  (323 shorter events, 130.8 us)
Async XLA Ops:
  7.2 121.1 %copy-start = (bf16[768,1536]{1,0:T(8,128)(2,1)S(1)}, bf16[768,1536]{1,0:T(8,128)(2,1)}, u32[]{:S(2)}) copy-start(bf16[768,1536]{1,0:T(8,128)(2,1)} %param.34) | copy-start | bytes 7077892
  7.2 6.4 copy-start.59
  7.2 6.4 copy-start.74
  7.2 6.4 copy-start.76
  7.2 111.2 %all-gather.5.cloned.1.call-start = ((), (), s32[]{:S(2)}) async-start(), calls=%async_computation.9 | async-start | bytes 9437184 | tf_op jit(solution)/shard_map/all_gather | solution.py:203
  9.7 3.9 copy-start.1
  19.1 5.1 copy-start.39
  19.1 5.0 copy-start.42
  19.4 4.8 copy-start.33
  19.4 4.8 copy-start.36
  37.6 16.7 %copy-start.25 = (bf16[2,512,6,64]{1,3,2,0:T(8,128)(2,1)S(1)}, bf16[2,512,6,64]{1,3,2,0:T(8,128)(2,1)}, u32[]{:S(2)}) copy-start(bf16[2,512,6,64]{1,3,2,0:T(8,128)(2,1)} %get-tuple-element.704) | copy-start | bytes 2359300 | tf_op jit(solution)/shard_map/while
  37.6 16.7 %copy-start.32 = (bf16[1024,6,64]{0,2,1:T(8,128)(2,1)S(1)}, bf16[1024,6,64]{0,2,1:T(8,128)(2,1)}, u32[]{:S(2)}) copy-start(bf16[1024,6,64]{0,2,1:T(8,128)(2,1)} %get-tuple-element.717) | copy-start | bytes 2359300 | tf_op jit(solution)/shard_map/while
  69.7 16.7 %copy-start.25 = (bf16[2,512,6,64]{1,3,2,0:T(8,128)(2,1)S(1)}, bf16[2,512,6,64]{1,3,2,0:T(8,128)(2,1)}, u32[]{:S(2)}) copy-start(bf16[2,512,6,64]{1,3,2,0:T(8,128)(2,1)} %get-tuple-element.704) | copy-start | bytes 2359300 | tf_op jit(solution)/shard_map/while
  69.7 16.7 %copy-start.32 = (bf16[1024,6,64]{0,2,1:T(8,128)(2,1)S(1)}, bf16[1024,6,64]{0,2,1:T(8,128)(2,1)}, u32[]{:S(2)}) copy-start(bf16[1024,6,64]{0,2,1:T(8,128)(2,1)} %get-tuple-element.717) | copy-start | bytes 2359300 | tf_op jit(solution)/shard_map/while
  98.8 75.6 %all-reduce.7.cloned.1.call-start = ((), (), s32[]{:S(2)}) async-start(), calls=%async_computation.3 | async-start | bytes 6291456 | tf_op jit(solution)/shard_map/psum | solution.py:216
  118.4 5.2 copy-start.49
  149.8 24.7 %copy-start.68 = (f32[768]{0:T(1024)S(1)}, f32[768]{0:T(1024)}, u32[]{:S(2)}) copy-start(f32[768]{0:T(1024)} %param.37) | copy-start | bytes 9220
  149.8 96.4 %all-gather.7.cloned.1.call-start = ((), (), s32[]{:S(2)}) async-start(), calls=%async_computation.10 | async-start | bytes 9437184 | tf_op jit(solution)/shard_map/all_gather | solution.py:203
  174.5 5.1 copy-start.3
  179.9 4.0 copy-start.45
  185.3 4.0 copy-start.14
  185.3 4.0 copy-start.15
  228.1 78.5 %all-reduce.9.cloned.1.call-start = ((), (), s32[]{:S(2)}) async-start(), calls=%async_computation.4 | async-start | bytes 6291456 | tf_op jit(solution)/shard_map/psum | solution.py:316
  254.3 15.9 %copy-start.9 = (f32[1024,768]{1,0:T(8,128)}, f32[1024,768]{1,0:T(8,128)S(1)}, u32[]{:S(2)}) copy-start(f32[1024,768]{1,0:T(8,128)S(1)} %get-tuple-element.484) | copy-start | bytes 9437188
  254.3 56.7 %copy-start.47 = (f32[1024]{0:T(1024)}, f32[1024]{0:T(1024)S(1)}, u32[]{:S(2)}) copy-start(f32[1024]{0:T(1024)S(1)} %broadcast_multiply_fusion.4) | copy-start | bytes 12292
  255.1 55.9 %copy-start.52 = (f32[1024]{0:T(1024)}, f32[1024]{0:T(1024)S(1)}, u32[]{:S(2)}) copy-start(f32[1024]{0:T(1024)S(1)} %add_rsqrt_fusion) | copy-start | bytes 12292
  255.1 15.1 %copy-start.31 = (bf16[1024,768]{1,0:T(8,128)(2,1)S(1)}, bf16[1024,768]{1,0:T(8,128)(2,1)}, u32[]{:S(2)}) copy-start(bf16[1024,768]{1,0:T(8,128)(2,1)} %param.24) | copy-start | bytes 4718596
  255.1 15.1 %copy-start.64 = (bf16[1024]{0:T(1024)(128)(2,1)S(1)}, bf16[1024]{0:T(1024)(128)(2,1)}, u32[]{:S(2)}) copy-start(bf16[1024]{0:T(1024)(128)(2,1)} %get-tuple-element.481) | copy-start | bytes 6148
  255.1 15.2 %copy-start.69 = (bf16[1536,768]{1,0:T(8,128)(2,1)S(1)}, bf16[1536,768]{1,0:T(8,128)(2,1)}, u32[]{:S(2)}) copy-start(bf16[1536,768]{1,0:T(8,128)(2,1)} %param.36) | copy-start | bytes 7077892
  270.2 5.7 copy-start.83
  270.2 5.7 copy-start.84
  282.0 209.6 %all-reduce.11.cloned.1.call-start = ((), (), s32[]{:S(2)}) async-start(), calls=%async_computation.5 | async-start | bytes 6291456 | tf_op jit(solution)/shard_map/psum | solution.py:348
  306.6 4.5 copy-start.10
  306.6 4.7 copy-start.16
  311.3 5.5 copy-start.22
  330.2 4.6 copy-start.13
  373.4 5.8 copy-start.13
  418.1 5.4 copy-start.6
  430.5 4.9 copy-start.27
  441.3 211.3 %all-reduce.13.cloned.1.call-start = ((), (), s32[]{:S(2)}) async-start(), calls=%async_computation.11 | async-start | bytes 9437184
  454.6 5.3 copy-start.65
  454.7 5.3 copy-start.73
  454.7 327.3 %reduce-scatter.4.cloned.1.call-start = ((), (), s32[]{:S(2)}) async-start(), calls=%async_computation.6 | async-start | bytes 1253376 | tf_op jit(solution)/shard_map/reduce_scatter | solution.py:357
  459.7 465.8 %reduce-scatter.8.cloned.1.call-start = ((), (), s32[]{:S(2)}) async-start(), calls=%async_computation.8 | async-start | bytes 5013504 | tf_op jit(solution)/shard_map/reduce_scatter | solution.py:359
  471.4 597.6 %reduce-scatter.6.cloned.1.call-start = ((), (), s32[]{:S(2)}) async-start(), calls=%async_computation.7 | async-start | bytes 5013504 | tf_op jit(solution)/shard_map/reduce_scatter | solution.py:358
  482.0 9.2 copy-start.28
  482.0 9.2 copy-start.29
  482.0 9.2 copy-start.30
  (58 other events, 109.7 us)
Sparse Core Ops, SparseCore 0:
  98.9 19.4 all-gather.4
  149.9 24.4 all-reduce.6
  228.2 17.9 all-gather.6
  282.1 24.4 all-reduce.8
  441.4 24.4 all-reduce.10
  471.5 181.0 all-reduce.12
  657.9 124.0 reduce-scatter.3
  787.7 137.6 reduce-scatter.7
  931.2 137.7 reduce-scatter.5
